TPU v7x, 32 devices: a whole 2x2x4 slice. The times are simulated.
32 devices in a mesh: pipe: 4 (over y, x), dp: 8 (over z, core).
Axes of the slice: x: 2, y: 2, z: 4, core: 2. Of those that a mesh axis runs over, the one named last changes fastest.
Arguments:
- inputs: bfloat16 [8, 4, 32, 8192], P('dp'), may hold values from -48 to 48
- segments: int32 [8, 4, 32], P('dp'), may hold values from 0 to 3, never falling along the last dimension, each value on 1 to 16 neighbouring positions
- cotangent: bfloat16 [8, 4, 32, 8192], P('dp'), may hold values from -6 to 6
- w_query: bfloat16 [4, 8192, 128], P('pipe', 'dp'), may hold values from -3 to 3
- w_key: bfloat16 [4, 8192, 128], P('pipe', 'dp'), may hold values from -3 to 3
- w_value: bfloat16 [4, 8192, 128], P('pipe', 'dp'), may hold values from -0.0625 to 0.0625
- w_out: bfloat16 [4, 8192, 128], P('pipe', 'dp'), may hold values from -0.5 to 0.5
Outputs:
- input_grads: bfloat16 [4, 8, 4, 32, 8192], P('pipe', 'dp')
- grad_query: float32 [4, 8192, 128], P('pipe', 'dp')
- grad_key: float32 [4, 8192, 128], P('pipe', 'dp')
- grad_value: float32 [4, 8192, 128], P('pipe', 'dp')
- grad_out: float32 [4, 8192, 128], P('pipe', 'dp')
Inputs may be any that keep to these rules, and one draw needn't show every extreme that they name: `segments`: along each micro-batch the numbers never fall; a document has 1 to 16 tokens, and one has exactly 16.
All inputs are finite; a program needn't handle non-finite values.
Results may differ from a plain program's by a relative error of at most 0.025.
Values may be sent and summed in bfloat16 or wider, within the bound.
No kernel may reach another device: no remote copies, remote signals or barrier semaphores. Data moves between devices by JAX's collectives and lax.ppermute only.
A program may use at most 192 MiB of HBM per device.

v0:
```python
import jax
import jax.numpy as jnp
from jax import lax
from jax.sharding import PartitionSpec as P


def shifted(block, axis, distance):
    devices = range(lax.axis_size(axis))
    route = [(i - distance, i) for i in devices if i - distance in devices]
    return lax.ppermute(block, axis, route)


def section(hidden, doc_ids, w_query, w_key, w_value, w_out):
    widen = hidden.astype(jnp.float32)
    normed = (widen * lax.rsqrt(jnp.mean(widen * widen, axis=-1, keepdims=True) + 1e-05)).astype(
        jnp.bfloat16
    )
    query = jnp.dot(normed, w_query, preferred_element_type=jnp.float32).astype(jnp.bfloat16)
    keys = jnp.dot(normed, w_key, preferred_element_type=jnp.float32).astype(jnp.bfloat16)
    values = jnp.dot(normed, w_value, preferred_element_type=jnp.float32).astype(jnp.bfloat16)
    scores = jnp.dot(query, keys.T, preferred_element_type=jnp.float32) * w_query.shape[1] ** (-0.5)
    places = jnp.arange(hidden.shape[0])
    allowed = (places[:, None] >= places[None, :]) & (doc_ids[:, None] == doc_ids[None, :])
    scores = jnp.where(allowed, scores, -1e30)
    highest = jnp.max(scores, axis=-1, keepdims=True)
    exponent = jnp.where(allowed, jnp.exp(scores - highest), 0.0)
    attend = (exponent / jnp.sum(exponent, axis=-1, keepdims=True)).astype(jnp.bfloat16)
    mixed = jnp.dot(attend, values, preferred_element_type=jnp.float32).astype(jnp.bfloat16)
    update = jnp.dot(mixed, w_out.T, preferred_element_type=jnp.float32)
    return (widen + update).astype(jnp.bfloat16)


def shards(inputs, segments, cotangent, w_query, w_key, w_value, w_out):
    sections = lax.axis_size("pipe")
    section_id = lax.axis_index("pipe")
    full_query, full_key, full_value, full_out = (
        lax.all_gather(w_query, "dp", axis=1, tiled=True),
        lax.all_gather(w_key, "dp", axis=1, tiled=True),
        lax.all_gather(w_value, "dp", axis=1, tiled=True),
        lax.all_gather(w_out, "dp", axis=1, tiled=True),
    )
    layer = (full_query[0], full_key[0], full_value[0], full_out[0])
    features = inputs[0]
    doc_table = segments[0]
    final_cots = cotangent[0]
    batches = features.shape[0]
    ticks = sections + batches - 1

    def forward_tick(tick, carry):
        incoming, stash = carry
        offset = tick - section_id
        active = (offset >= 0) & (offset < batches)
        batch_slot = jnp.clip(offset, 0, batches - 1)
        first = lax.dynamic_index_in_dim(features, batch_slot, 0, keepdims=False)
        section_input = jnp.where(section_id == 0, first, incoming)
        doc_ids = lax.dynamic_index_in_dim(doc_table, batch_slot, 0, keepdims=False)
        result = lax.cond(
            active,
            lambda: section(section_input, doc_ids, *layer),
            lambda: jnp.zeros_like(section_input),
        )
        previous = lax.dynamic_index_in_dim(stash, batch_slot, 0, keepdims=False)
        stash = lax.dynamic_update_index_in_dim(
            stash, jnp.where(active, section_input, previous), batch_slot, 0
        )
        incoming = shifted(result, "pipe", 1)
        return (incoming, stash)

    start_buffer = jnp.zeros(features.shape[1:], jnp.bfloat16)
    _, stash = lax.fori_loop(0, ticks, forward_tick, (start_buffer, jnp.zeros_like(features)))

    def backward_tick(tick, carry):
        incoming, totals, stored = carry
        offset = tick - (sections - 1 - section_id)
        active = (offset >= 0) & (offset < batches)
        batch_slot = jnp.clip(offset, 0, batches - 1)
        last_cot = lax.dynamic_index_in_dim(final_cots, batch_slot, 0, keepdims=False)
        grad_input = jnp.where(section_id == sections - 1, last_cot, incoming)
        saved_h = lax.dynamic_index_in_dim(stash, batch_slot, 0, keepdims=False)
        doc_ids = lax.dynamic_index_in_dim(doc_table, batch_slot, 0, keepdims=False)

        def run_back():
            _, pull = jax.vjp(
                lambda hid, wa, wb, wc, wd: section(hid, doc_ids, wa, wb, wc, wd), saved_h, *layer
            )
            outs = pull(grad_input)
            return (outs[0], tuple((grad.astype(jnp.float32) for grad in outs[1:])))

        def skip_back():
            return (
                jnp.zeros_like(saved_h),
                tuple((jnp.zeros(part.shape, jnp.float32) for part in layer)),
            )

        cot_input, parts = lax.cond(active, run_back, skip_back)
        totals = tuple((total + part for total, part in zip(totals, parts)))
        previous = lax.dynamic_index_in_dim(stored, batch_slot, 0, keepdims=False)
        stored = lax.dynamic_update_index_in_dim(
            stored, jnp.where(active, cot_input, previous), batch_slot, 0
        )
        incoming = shifted(cot_input, "pipe", -1)
        return (incoming, totals, stored)

    zero_totals = tuple((jnp.zeros(part.shape, jnp.float32) for part in layer))
    _, totals, stored = lax.fori_loop(
        0, ticks, backward_tick, (start_buffer, zero_totals, jnp.zeros_like(features))
    )
    owned_grads = (
        lax.psum_scatter(
            totals[0].astype(jnp.bfloat16)[None], "dp", scatter_dimension=1, tiled=True
        ).astype(jnp.float32),
        lax.psum_scatter(
            totals[1].astype(jnp.bfloat16)[None], "dp", scatter_dimension=1, tiled=True
        ).astype(jnp.float32),
        lax.psum_scatter(
            totals[2].astype(jnp.bfloat16)[None], "dp", scatter_dimension=1, tiled=True
        ).astype(jnp.float32),
        lax.psum_scatter(
            totals[3].astype(jnp.bfloat16)[None], "dp", scatter_dimension=1, tiled=True
        ).astype(jnp.float32),
    )
    return (stored[None, None], owned_grads[0], owned_grads[1], owned_grads[2], owned_grads[3])


def solution(mesh):
    placed = (
        P("dp", None, None, None),
        P("dp", None, None),
        P("dp", None, None, None),
        P("pipe", "dp", None),
        P("pipe", "dp", None),
        P("pipe", "dp", None),
        P("pipe", "dp", None),
    )
    return jax.shard_map(
        shards,
        mesh=mesh,
        in_specs=placed,
        out_specs=(
            P("pipe", "dp", None, None, None),
            P("pipe", "dp", None),
            P("pipe", "dp", None),
            P("pipe", "dp", None),
            P("pipe", "dp", None),
        ),
        check_vma=False,
    )
```

profile of v0, /device:TPU:0, one launch (start us, length us, event | category | flops | bytes accessed | tf_op | source)
XLA Modules:
  0.0 771.5 jit_solution(6863091489487590063)
XLA Ops:
  10.1 31.4 %all-gather.5.cloned.1.call-done = bf16[1,8192,128]{2,1,0:T(8,128)(2,1)} async-done(((bf16[1,1024,128]{2,1,0:T(8,128)(2,1)}), bf16[1,8192,128]{2,1,0:T(8,128)(2,1)}) %all-gather.5.cloned.1.call-update) | async-done | bytes 2097168 | tf_op jit(solution)/shard_map/all_gather | solution.py:37
  41.4 30.2 %all-gather.7.cloned.1.call-done = bf16[1,8192,128]{2,1,0:T(8,128)(2,1)} async-done(((bf16[1,1024,128]{2,1,0:T(8,128)(2,1)}), bf16[1,8192,128]{2,1,0:T(8,128)(2,1)}) %all-gather.7.cloned.1.call-update) | async-done | bytes 2097168 | tf_op jit(solution)/shard_map/all_gather | solution.py:38
  71.7 30.2 %all-gather.9.cloned.1.call-done = bf16[1,8192,128]{2,1,0:T(8,128)(2,1)} async-done(((bf16[1,1024,128]{2,1,0:T(8,128)(2,1)}), bf16[1,8192,128]{2,1,0:T(8,128)(2,1)}) %all-gather.9.cloned.1.call-update) | async-done | bytes 2097168 | tf_op jit(solution)/shard_map/all_gather | solution.py:39
  101.9 30.1 %all-gather.11.cloned.1.call-done = bf16[1,8192,128]{2,1,0:T(8,128)(2,1)} async-done(((bf16[1,1024,128]{2,1,0:T(8,128)(2,1)}), bf16[1,8192,128]{2,1,0:T(8,128)(2,1)}) %all-gather.11.cloned.1.call-update) | async-done | bytes 2097168 | tf_op jit(solution)/shard_map/all_gather | solution.py:40
  133.6 171.1 %while.42 = (s32[]{:T(128)}, bf16[32,8192]{1,0:T(8,128)(2,1)S(1)}, bf16[4,32,8192]{2,1,0:T(8,128)(2,1)}, s32[]{:T(128)}, pred[]{:T(512)}, /*index=5*/bf16[4,32,8...) while((s32[]{:T(128)}, bf16[32,8192]{1,0:T(8,128)(2,1)S(1)}, ...), condition=%wide.region_6.7_spmd, body=%wide.region_0.6_spmd.sunk | while | flops 273452000 | bytes 19447128 | solution.py:70
  146.7 12.1 %collective-permute-done = bf16[32,8192]{1,0:T(8,128)(2,1)S(1)} collective-permute-done((bf16[32,8192]{1,0:T(8,128)(2,1)}, bf16[32,8192]{1,0:T(8,128)(2,1)S(1)}, u32[]{:S(2)}, u32[]{:S(2)}) %collective-permute-start) | collective-permute-done | bytes 524320 | tf_op jit(solution)/shard_map/while/body/eval_jaxpr/ppermute | solution.py:10
  174.8 11.3 %collective-permute-done = bf16[32,8192]{1,0:T(8,128)(2,1)S(1)} collective-permute-done((bf16[32,8192]{1,0:T(8,128)(2,1)}, bf16[32,8192]{1,0:T(8,128)(2,1)S(1)}, u32[]{:S(2)}, u32[]{:S(2)}) %collective-permute-start) | collective-permute-done | bytes 524320 | tf_op jit(solution)/shard_map/while/body/eval_jaxpr/ppermute | solution.py:10
  202.1 10.5 %collective-permute-done = bf16[32,8192]{1,0:T(8,128)(2,1)S(1)} collective-permute-done((bf16[32,8192]{1,0:T(8,128)(2,1)}, bf16[32,8192]{1,0:T(8,128)(2,1)S(1)}, u32[]{:S(2)}, u32[]{:S(2)}) %collective-permute-start) | collective-permute-done | bytes 524320 | tf_op jit(solution)/shard_map/while/body/eval_jaxpr/ppermute | solution.py:10
  242.1 12.4 %collective-permute-start = (bf16[32,8192]{1,0:T(8,128)(2,1)}, bf16[32,8192]{1,0:T(8,128)(2,1)S(1)}, u32[]{:S(2)}, u32[]{:S(2)}) collective-permute-start(bf16[32,8192]{1,0:T(8,128)(2,1)} %copy-done.9), channel_id=1, source_target_pairs={{0,8},{8,16},{16,24},{1,9},{9,17},{17,25},{2,10},{10,18},{18,26},{... | collective-permute-start | bytes 1572872 | tf_op jit(solution)/shard_map/while/body/eval_jaxpr/ppermute | solution.py:10
  284.7 12.9 %collective-permute-start = (bf16[32,8192]{1,0:T(8,128)(2,1)}, bf16[32,8192]{1,0:T(8,128)(2,1)S(1)}, u32[]{:S(2)}, u32[]{:S(2)}) collective-permute-start(bf16[32,8192]{1,0:T(8,128)(2,1)} %copy-done.9), channel_id=1, source_target_pairs={{0,8},{8,16},{16,24},{1,9},{9,17},{17,25},{2,10},{10,18},{18,26},{... | collective-permute-start | bytes 1572872 | tf_op jit(solution)/shard_map/while/body/eval_jaxpr/ppermute | solution.py:10
  307.0 305.3 %while.43 = (s32[]{:T(128)}, bf16[32,8192]{1,0:T(8,128)(2,1)}, f32[8192,128]{1,0:T(8,128)}, f32[8192,128]{1,0:T(8,128)}, f32[8192,128]{1,0:T(8,128)}, /*index=5*...) while((s32[]{:T(128)}, bf16[32,8192]{1,0:T(8,128)(2,1)}, ...), condition=%wide.region_17.18_spmd.clone, body=%wide.region_7.17_spmd.clone.sunk | while | flops 767129792 | bytes 153846560 | solution.py:105
  346.4 9.9 %select_add_fusion.7 = (f32[8192,128]{1,0:T(8,128)}, f32[8192,128]{1,0:T(8,128)}) fusion(f32[8192,128]{1,0:T(8,128)} %get-tuple-element.1022, f32[8192,128]{1,0:T(8,128)} %get-tuple-element.1106, pred[]{:T(512)S(6)} %compare.3, f32[8192,128]{1,0:T(8,128)} %get-tuple-element.1023, f32[8192,128]{1,0:T(8,128)} %get-tuple-element.1105), kind=kLoop, calls=%fused_computation.93.clone.1 | loop fusion | flops 4194304 | bytes 25165824 | tf_op jit(solution)/shard_map/while/body/eval_jaxpr/add | solution.py:96
  379.3 9.9 %select_add_fusion.7 = (f32[8192,128]{1,0:T(8,128)}, f32[8192,128]{1,0:T(8,128)}) fusion(f32[8192,128]{1,0:T(8,128)} %get-tuple-element.1022, f32[8192,128]{1,0:T(8,128)} %get-tuple-element.1106, pred[]{:T(512)S(6)} %compare.3, f32[8192,128]{1,0:T(8,128)} %get-tuple-element.1023, f32[8192,128]{1,0:T(8,128)} %get-tuple-element.1105), kind=kLoop, calls=%fused_computation.93.clone.1 | loop fusion | flops 4194304 | bytes 25165824 | tf_op jit(solution)/shard_map/while/body/eval_jaxpr/add | solution.py:96
  400.0 19.2 %collective-permute-done.1 = bf16[32,8192]{1,0:T(8,128)(2,1)S(1)} collective-permute-done((bf16[32,8192]{1,0:T(8,128)(2,1)S(1)}, bf16[32,8192]{1,0:T(8,128)(2,1)S(1)}, u32[]{:S(2)}, u32[]{:S(2)}) %collective-permute-start.1) | collective-permute-done | bytes 524320 | tf_op jit(solution)/shard_map/while/body/eval_jaxpr/ppermute | solution.py:10
  420.0 23.7 %conditional.6 = (bf16[32,8192]{1,0:T(8,128)(2,1)S(1)}, f32[8192,128]{1,0:T(8,128)}, f32[8192,128]{1,0:T(8,128)}, f32[8192,128]{1,0:T(8,128)}, f32[8192,128]{1,0:T(8,128)}) conditional(s32[]{:T(128)} %convert_element_type.326, () %tuple.115, (pred[]{:T(512)}, bf16[4,32,8192]{2,1,0:T(8,128)(2,1)}, s32[]{:T(128)}, bf16[32,8192]{1,0:T(8,128)(2,1)}, ...), branch_computations={%region_8.8_spmd, %region_9.16_spmd} | conditional | flops 758479040 | bytes 96698248 | solution.py:95
  446.1 9.9 %select_add_fusion.7 = (f32[8192,128]{1,0:T(8,128)}, f32[8192,128]{1,0:T(8,128)}) fusion(f32[8192,128]{1,0:T(8,128)} %get-tuple-element.1022, f32[8192,128]{1,0:T(8,128)} %get-tuple-element.1106, pred[]{:T(512)S(6)} %compare.3, f32[8192,128]{1,0:T(8,128)} %get-tuple-element.1023, f32[8192,128]{1,0:T(8,128)} %get-tuple-element.1105), kind=kLoop, calls=%fused_computation.93.clone.1 | loop fusion | flops 4194304 | bytes 25165824 | tf_op jit(solution)/shard_map/while/body/eval_jaxpr/add | solution.py:96
  468.2 23.7 %conditional.6 = (bf16[32,8192]{1,0:T(8,128)(2,1)S(1)}, f32[8192,128]{1,0:T(8,128)}, f32[8192,128]{1,0:T(8,128)}, f32[8192,128]{1,0:T(8,128)}, f32[8192,128]{1,0:T(8,128)}) conditional(s32[]{:T(128)} %convert_element_type.326, () %tuple.115, (pred[]{:T(512)}, bf16[4,32,8192]{2,1,0:T(8,128)(2,1)}, s32[]{:T(128)}, bf16[32,8192]{1,0:T(8,128)(2,1)}, ...), branch_computations={%region_8.8_spmd, %region_9.16_spmd} | conditional | flops 758479040 | bytes 96698248 | solution.py:95
  494.3 9.9 %select_add_fusion.7 = (f32[8192,128]{1,0:T(8,128)}, f32[8192,128]{1,0:T(8,128)}) fusion(f32[8192,128]{1,0:T(8,128)} %get-tuple-element.1022, f32[8192,128]{1,0:T(8,128)} %get-tuple-element.1106, pred[]{:T(512)S(6)} %compare.3, f32[8192,128]{1,0:T(8,128)} %get-tuple-element.1023, f32[8192,128]{1,0:T(8,128)} %get-tuple-element.1105), kind=kLoop, calls=%fused_computation.93.clone.1 | loop fusion | flops 4194304 | bytes 25165824 | tf_op jit(solution)/shard_map/while/body/eval_jaxpr/add | solution.py:96
  516.5 23.7 %conditional.6 = (bf16[32,8192]{1,0:T(8,128)(2,1)S(1)}, f32[8192,128]{1,0:T(8,128)}, f32[8192,128]{1,0:T(8,128)}, f32[8192,128]{1,0:T(8,128)}, f32[8192,128]{1,0:T(8,128)}) conditional(s32[]{:T(128)} %convert_element_type.326, () %tuple.115, (pred[]{:T(512)}, bf16[4,32,8192]{2,1,0:T(8,128)(2,1)}, s32[]{:T(128)}, bf16[32,8192]{1,0:T(8,128)(2,1)}, ...), branch_computations={%region_8.8_spmd, %region_9.16_spmd} | conditional | flops 758479040 | bytes 96698248 | solution.py:95
  564.7 23.7 %conditional.6 = (bf16[32,8192]{1,0:T(8,128)(2,1)S(1)}, f32[8192,128]{1,0:T(8,128)}, f32[8192,128]{1,0:T(8,128)}, f32[8192,128]{1,0:T(8,128)}, f32[8192,128]{1,0:T(8,128)}) conditional(s32[]{:T(128)} %convert_element_type.326, () %tuple.115, (pred[]{:T(512)}, bf16[4,32,8192]{2,1,0:T(8,128)(2,1)}, s32[]{:T(128)}, bf16[32,8192]{1,0:T(8,128)(2,1)}, ...), branch_computations={%region_8.8_spmd, %region_9.16_spmd} | conditional | flops 758479040 | bytes 96698248 | solution.py:95
  627.4 25.3 %reduce-scatter.5.cloned.1.call-done = bf16[1,1024,128]{2,1,0:T(8,128)(2,1)} async-done(((bf16[1,8192,128]{2,1,0:T(8,128)(2,1)}), bf16[1,1024,128]{2,1,0:T(8,128)(2,1)}) %reduce-scatter.5.cloned.1.call-update) | async-done | bytes 262160 | tf_op jit(solution)/shard_map/reduce_scatter | solution.py:109
  654.5 34.9 %reduce-scatter.7.cloned.1.call-done = bf16[1,1024,128]{2,1,0:T(8,128)(2,1)} async-done(((bf16[1,8192,128]{2,1,0:T(8,128)(2,1)}), bf16[1,1024,128]{2,1,0:T(8,128)(2,1)}) %reduce-scatter.7.cloned.1.call-update) | async-done | bytes 262160 | tf_op jit(solution)/shard_map/reduce_scatter | solution.py:112
  691.2 35.0 %reduce-scatter.9.cloned.1.call-done = bf16[1,1024,128]{2,1,0:T(8,128)(2,1)} async-done(((bf16[1,8192,128]{2,1,0:T(8,128)(2,1)}), bf16[1,1024,128]{2,1,0:T(8,128)(2,1)}) %reduce-scatter.9.cloned.1.call-update) | async-done | bytes 262160 | tf_op jit(solution)/shard_map/reduce_scatter | solution.py:115
  727.9 35.0 %reduce-scatter.11.cloned.1.call-done = bf16[1,1024,128]{2,1,0:T(8,128)(2,1)} async-done(((bf16[1,8192,128]{2,1,0:T(8,128)(2,1)}), bf16[1,1024,128]{2,1,0:T(8,128)(2,1)}) %reduce-scatter.11.cloned.1.call-update) | async-done | bytes 262160 | tf_op jit(solution)/shard_map/reduce_scatter | solution.py:118
  (348 shorter events, 443.9 us)
Async XLA Ops:
  7.2 126.4 %copy-start.10 = (s32[1,4,32]{2,1,0:T(4,128)S(1)}, s32[1,4,32]{2,1,0:T(4,128)}, u32[]{:S(2)}) copy-start(s32[1,4,32]{2,1,0:T(4,128)} %param.16) | copy-start | bytes 1540
  7.2 34.3 %all-gather.5.cloned.1.call-start = ((), (), s32[]{:S(2)}) async-start(), calls=%async_computation.4 | async-start | bytes 2359296 | tf_op jit(solution)/shard_map/all_gather | solution.py:37
  7.9 63.8 %all-gather.7.cloned.1.call-start = ((), (), s32[]{:S(2)}) async-start(), calls=%async_computation.5 | async-start | bytes 2359296 | tf_op jit(solution)/shard_map/all_gather | solution.py:38
  8.7 93.2 %all-gather.9.cloned.1.call-start = ((), (), s32[]{:S(2)}) async-start(), calls=%async_computation.6 | async-start | bytes 2359296 | tf_op jit(solution)/shard_map/all_gather | solution.py:39
  9.4 122.6 %all-gather.11.cloned.1.call-start = ((), (), s32[]{:S(2)}) async-start(), calls=%async_computation.7 | async-start | bytes 2359296 | tf_op jit(solution)/shard_map/all_gather | solution.py:40
  10.0 642.8 %reduce-scatter.5.cloned.1.call-start = ((), (), s32[]{:S(2)}) async-start(), calls=%async_computation.8 | async-start | bytes 2359296 | tf_op jit(solution)/shard_map/reduce_scatter | solution.py:109
  41.4 92.1 %copy-start = (bf16[1,8192,128]{2,1,0:T(8,128)(2,1)S(1)}, bf16[1,8192,128]{2,1,0:T(8,128)(2,1)}, u32[]{:S(2)}) copy-start(bf16[1,8192,128]{2,1,0:T(8,128)(2,1)} %all-gather.5.cloned.1.call-done) | copy-start | bytes 6291460
  145.3 13.4 %collective-permute-start = (bf16[32,8192]{1,0:T(8,128)(2,1)}, bf16[32,8192]{1,0:T(8,128)(2,1)S(1)}, u32[]{:S(2)}, u32[]{:S(2)}) collective-permute-start(bf16[32,8192]{1,0:T(8,128)(2,1)} %copy-done.9), channel_id=1, source_target_pairs={{0,8},{8,16},{16,24},{1,9},{9,17},{17,25},{2,10},{10,18},{18,26},{... | collective-permute-start | bytes 1572872 | tf_op jit(solution)/shard_map/while/body/eval_jaxpr/ppermute | solution.py:10
  170.4 15.7 %collective-permute-start = (bf16[32,8192]{1,0:T(8,128)(2,1)}, bf16[32,8192]{1,0:T(8,128)(2,1)S(1)}, u32[]{:S(2)}, u32[]{:S(2)}) collective-permute-start(bf16[32,8192]{1,0:T(8,128)(2,1)} %copy-done.9), channel_id=1, source_target_pairs={{0,8},{8,16},{16,24},{1,9},{9,17},{17,25},{2,10},{10,18},{18,26},{... | collective-permute-start | bytes 1572872 | tf_op jit(solution)/shard_map/while/body/eval_jaxpr/ppermute | solution.py:10
  197.8 14.7 %collective-permute-start = (bf16[32,8192]{1,0:T(8,128)(2,1)}, bf16[32,8192]{1,0:T(8,128)(2,1)S(1)}, u32[]{:S(2)}, u32[]{:S(2)}) collective-permute-start(bf16[32,8192]{1,0:T(8,128)(2,1)} %copy-done.9), channel_id=1, source_target_pairs={{0,8},{8,16},{16,24},{1,9},{9,17},{17,25},{2,10},{10,18},{18,26},{... | collective-permute-start | bytes 1572872 | tf_op jit(solution)/shard_map/while/body/eval_jaxpr/ppermute | solution.py:10
  224.3 13.8 %collective-permute-start = (bf16[32,8192]{1,0:T(8,128)(2,1)}, bf16[32,8192]{1,0:T(8,128)(2,1)S(1)}, u32[]{:S(2)}, u32[]{:S(2)}) collective-permute-start(bf16[32,8192]{1,0:T(8,128)(2,1)} %copy-done.9), channel_id=1, source_target_pairs={{0,8},{8,16},{16,24},{1,9},{9,17},{17,25},{2,10},{10,18},{18,26},{... | collective-permute-start | bytes 1572872 | tf_op jit(solution)/shard_map/while/body/eval_jaxpr/ppermute | solution.py:10
  242.1 21.3 %collective-permute-start = (bf16[32,8192]{1,0:T(8,128)(2,1)}, bf16[32,8192]{1,0:T(8,128)(2,1)S(1)}, u32[]{:S(2)}, u32[]{:S(2)}) collective-permute-start(bf16[32,8192]{1,0:T(8,128)(2,1)} %copy-done.9), channel_id=1, source_target_pairs={{0,8},{8,16},{16,24},{1,9},{9,17},{17,25},{2,10},{10,18},{18,26},{... | collective-permute-start | bytes 1572872 | tf_op jit(solution)/shard_map/while/body/eval_jaxpr/ppermute | solution.py:10
  267.5 13.2 %collective-permute-start = (bf16[32,8192]{1,0:T(8,128)(2,1)}, bf16[32,8192]{1,0:T(8,128)(2,1)S(1)}, u32[]{:S(2)}, u32[]{:S(2)}) collective-permute-start(bf16[32,8192]{1,0:T(8,128)(2,1)} %copy-done.9), channel_id=1, source_target_pairs={{0,8},{8,16},{16,24},{1,9},{9,17},{17,25},{2,10},{10,18},{18,26},{... | collective-permute-start | bytes 1572872 | tf_op jit(solution)/shard_map/while/body/eval_jaxpr/ppermute | solution.py:10
  284.7 20.0 %collective-permute-start = (bf16[32,8192]{1,0:T(8,128)(2,1)}, bf16[32,8192]{1,0:T(8,128)(2,1)S(1)}, u32[]{:S(2)}, u32[]{:S(2)}) collective-permute-start(bf16[32,8192]{1,0:T(8,128)(2,1)} %copy-done.9), channel_id=1, source_target_pairs={{0,8},{8,16},{16,24},{1,9},{9,17},{17,25},{2,10},{10,18},{18,26},{... | collective-permute-start | bytes 1572872 | tf_op jit(solution)/shard_map/while/body/eval_jaxpr/ppermute | solution.py:10
  315.9 18.3 %collective-permute-start.1 = (bf16[32,8192]{1,0:T(8,128)(2,1)S(1)}, bf16[32,8192]{1,0:T(8,128)(2,1)S(1)}, u32[]{:S(2)}, u32[]{:S(2)}) collective-permute-start(bf16[32,8192]{1,0:T(8,128)(2,1)S(1)} %get-tuple-element.1017), channel_id=1, source_target_pairs={{8,0},{16,8},{24,16},{9,1},{17,9},{25,17},{10,2},{18,10},{26,18},{... | collective-permute-start | bytes 1572872 | tf_op jit(solution)/shard_map/while/body/eval_jaxpr/ppermute | solution.py:10
  344.0 23.1 %collective-permute-start.1 = (bf16[32,8192]{1,0:T(8,128)(2,1)S(1)}, bf16[32,8192]{1,0:T(8,128)(2,1)S(1)}, u32[]{:S(2)}, u32[]{:S(2)}) collective-permute-start(bf16[32,8192]{1,0:T(8,128)(2,1)S(1)} %get-tuple-element.1017), channel_id=1, source_target_pairs={{8,0},{16,8},{24,16},{9,1},{17,9},{25,17},{10,2},{18,10},{26,18},{... | collective-permute-start | bytes 1572872 | tf_op jit(solution)/shard_map/while/body/eval_jaxpr/ppermute | solution.py:10
  376.9 42.3 %collective-permute-start.1 = (bf16[32,8192]{1,0:T(8,128)(2,1)S(1)}, bf16[32,8192]{1,0:T(8,128)(2,1)S(1)}, u32[]{:S(2)}, u32[]{:S(2)}) collective-permute-start(bf16[32,8192]{1,0:T(8,128)(2,1)S(1)} %get-tuple-element.1017), channel_id=1, source_target_pairs={{8,0},{16,8},{24,16},{9,1},{17,9},{25,17},{10,2},{18,10},{26,18},{... | collective-permute-start | bytes 1572872 | tf_op jit(solution)/shard_map/while/body/eval_jaxpr/ppermute | solution.py:10
  443.7 23.7 %collective-permute-start.1 = (bf16[32,8192]{1,0:T(8,128)(2,1)S(1)}, bf16[32,8192]{1,0:T(8,128)(2,1)S(1)}, u32[]{:S(2)}, u32[]{:S(2)}) collective-permute-start(bf16[32,8192]{1,0:T(8,128)(2,1)S(1)} %get-tuple-element.1017), channel_id=1, source_target_pairs={{8,0},{16,8},{24,16},{9,1},{17,9},{25,17},{10,2},{18,10},{26,18},{... | collective-permute-start | bytes 1572872 | tf_op jit(solution)/shard_map/while/body/eval_jaxpr/ppermute | solution.py:10
  491.9 23.7 %collective-permute-start.1 = (bf16[32,8192]{1,0:T(8,128)(2,1)S(1)}, bf16[32,8192]{1,0:T(8,128)(2,1)S(1)}, u32[]{:S(2)}, u32[]{:S(2)}) collective-permute-start(bf16[32,8192]{1,0:T(8,128)(2,1)S(1)} %get-tuple-element.1017), channel_id=1, source_target_pairs={{8,0},{16,8},{24,16},{9,1},{17,9},{25,17},{10,2},{18,10},{26,18},{... | collective-permute-start | bytes 1572872 | tf_op jit(solution)/shard_map/while/body/eval_jaxpr/ppermute | solution.py:10
  540.1 23.7 %collective-permute-start.1 = (bf16[32,8192]{1,0:T(8,128)(2,1)S(1)}, bf16[32,8192]{1,0:T(8,128)(2,1)S(1)}, u32[]{:S(2)}, u32[]{:S(2)}) collective-permute-start(bf16[32,8192]{1,0:T(8,128)(2,1)S(1)} %get-tuple-element.1017), channel_id=1, source_target_pairs={{8,0},{16,8},{24,16},{9,1},{17,9},{25,17},{10,2},{18,10},{26,18},{... | collective-permute-start | bytes 1572872 | tf_op jit(solution)/shard_map/while/body/eval_jaxpr/ppermute | solution.py:10
  588.4 23.1 %collective-permute-start.1 = (bf16[32,8192]{1,0:T(8,128)(2,1)S(1)}, bf16[32,8192]{1,0:T(8,128)(2,1)S(1)}, u32[]{:S(2)}, u32[]{:S(2)}) collective-permute-start(bf16[32,8192]{1,0:T(8,128)(2,1)S(1)} %get-tuple-element.1017), channel_id=1, source_target_pairs={{8,0},{16,8},{24,16},{9,1},{17,9},{25,17},{10,2},{18,10},{26,18},{... | collective-permute-start | bytes 1572872 | tf_op jit(solution)/shard_map/while/body/eval_jaxpr/ppermute | solution.py:10
  616.0 73.4 %reduce-scatter.7.cloned.1.call-start = ((), (), s32[]{:S(2)}) async-start(), calls=%async_computation.9 | async-start | bytes 2359296 | tf_op jit(solution)/shard_map/reduce_scatter | solution.py:112
  619.8 106.3 %reduce-scatter.9.cloned.1.call-start = ((), (), s32[]{:S(2)}) async-start(), calls=%async_computation.10 | async-start | bytes 2359296 | tf_op jit(solution)/shard_map/reduce_scatter | solution.py:115
  623.6 139.3 %reduce-scatter.11.cloned.1.call-start = ((), (), s32[]{:S(2)}) async-start(), calls=%async_computation.11 | async-start | bytes 2359296 | tf_op jit(solution)/shard_map/reduce_scatter | solution.py:118
  (42 other events, 82.4 us)
Sparse Core Ops, SparseCore 0:
  9.6 31.7 all-gather.4
  43.0 28.5 all-gather.6
  73.3 28.5 all-gather.8
  103.4 28.5 all-gather.10
  616.1 36.5 reduce-scatter.4
  654.9 34.4 reduce-scatter.6
  691.7 34.4 reduce-scatter.8
  728.4 34.4 reduce-scatter.10
where the time goes:
time: 774 us; the launch traced here: 772 us
  waiting for transfers between devices  343 us (44%)
  other arithmetic  191 us (25%)
  matrix products  108 us (14%)
  local copies, waits for them, and re-layouts  59.5 us (8%)
  starting transfers between devices  54.1 us (7%)
  between operations  14.2 us (2%)
    add x14, other arithmetic, backward_tick(): totals = tuple((total + part for total, part in zip(totals, parts)))  134 us
    ppermute x14, waiting for transfers between devices, shifted(): return lax.ppermute(block, axis, route)  88.6 us
    ppermute x14, starting transfers between devices, shifted(): return lax.ppermute(block, axis, route)  53.8 us
    reduce_scatter x1, waiting for transfers between devices, shards(): lax.psum_scatter(totals[3].astype(jnp.bfloat16)[None], 'dp', scatter_dime...  35 us
    reduce_scatter x1, waiting for transfers between devices, shards(): lax.psum_scatter(totals[2].astype(jnp.bfloat16)[None], 'dp', scatter_dime...  35 us
    reduce_scatter x1, waiting for transfers between devices, shards(): lax.psum_scatter(totals[1].astype(jnp.bfloat16)[None], 'dp', scatter_dime...  34.9 us
    dot_general x16, matrix products, section(): jnp.dot(normed, w_key, preferred_element_type=jnp.float32)  32.3 us
    all_gather x1, waiting for transfers between devices, shards(): lax.all_gather(w_query, 'dp', axis=1, tiled=True)  31.4 us
  transfers between devices with their start and end apart: 22, of which 19 were waited for; matrix products, arithmetic and copies ran while one was open for 21% of the time, Pallas kernels for 0%

commit v1 on v0

--- a/solution.py
+++ b/solution.py
@@ -2,6 +2,27 @@
 import jax.numpy as jnp
 from jax import lax
 from jax.sharding import PartitionSpec as P
+
+
+def collect(array, axis, dim):
+    count, index, span = (lax.axis_size(axis), lax.axis_index(axis), array.shape[dim])
+    right = [(i, (i + 1) % count) for i in range(count)]
+    downward = [(i, (i - 1) % count) for i in range(count)]
+    filled = jnp.zeros((*array.shape[:dim], count * span, *array.shape[dim + 1 :]), array.dtype)
+    filled = lax.dynamic_update_slice_in_dim(filled, array, index * span, axis=dim)
+    from_left = from_right = array
+    middle = count // 2
+    for step in range(1, middle + 1):
+        from_left = lax.ppermute(from_left, axis, right)
+        filled = lax.dynamic_update_slice_in_dim(
+            filled, from_left, (index - step) % count * span, axis=dim
+        )
+        if step < count - middle:
+            from_right = lax.ppermute(from_right, axis, downward)
+            filled = lax.dynamic_update_slice_in_dim(
+                filled, from_right, (index + step) % count * span, axis=dim
+            )
+    return filled
 
 
 def shifted(block, axis, distance):
@@ -37,7 +58,7 @@
         lax.all_gather(w_query, "dp", axis=1, tiled=True),
         lax.all_gather(w_key, "dp", axis=1, tiled=True),
         lax.all_gather(w_value, "dp", axis=1, tiled=True),
-        lax.all_gather(w_out, "dp", axis=1, tiled=True),
+        collect(w_out, "dp", 1),
     )
     layer = (full_query[0], full_key[0], full_value[0], full_out[0])
     features = inputs[0]

time: 774 us -> 762 us (0.984)
  waiting for transfers between devices: 343 us -> 306 us
  starting transfers between devices: 54.1 us -> 66.1 us
    all_gather x1, waiting for transfers between devices: 31.4 us -> 0.01 us  [shards(): lax.all_gather(w_query, 'dp', axis=1, tiled=True)]
    all_gather x1 -> x0, waiting for transfers between devices: 30.1 us -> none  [shards(): lax.all_gather(w_out, 'dp', axis=1, tiled=True)]
    ppermute x0 -> x7, waiting for transfers between devices: none -> 26 us  [the longest x4 17.8 us: collect(): from_left = lax.ppermute(from_left, axis, right)]
    ppermute x0 -> x7, starting transfers between devices: none -> 12.1 us  [the longest x3 11.6 us: collect(): from_right = lax.ppermute(from_right, axis, downward)]
  transfers between devices with their start and end apart: 22 -> 28, of which waited for: 19 -> 24; matrix products, arithmetic and copies ran while one was open for 21% -> 23% of each run, Pallas kernels for 0% -> 0%
where the time goes in v1:
time: 762 us; the launch traced here: 759 us
  waiting for transfers between devices  306 us (40%)
  other arithmetic  190 us (25%)
  matrix products  115 us (15%)
  local copies, waits for them, and re-layouts  66.8 us (9%)
  starting transfers between devices  66.1 us (9%)
  between operations  14.2 us (2%)
    add x14, other arithmetic, backward_tick(): totals = tuple((total + part for total, part in zip(totals, parts)))  134 us
    ppermute x14, waiting for transfers between devices, shifted(): return lax.ppermute(block, axis, route)  92.9 us
    ppermute x14, starting transfers between devices, shifted(): return lax.ppermute(block, axis, route)  53.7 us
    reduce_scatter x1, waiting for transfers between devices, shards(): lax.psum_scatter(totals[3].astype(jnp.bfloat16)[None], 'dp', scatter_dime...  35 us
    reduce_scatter x1, waiting for transfers between devices, shards(): lax.psum_scatter(totals[1].astype(jnp.bfloat16)[None], 'dp', scatter_dime...  34.7 us
    reduce_scatter x1, waiting for transfers between devices, shards(): lax.psum_scatter(totals[2].astype(jnp.bfloat16)[None], 'dp', scatter_dime...  34.6 us
    dot_general x16, matrix products, section(): jnp.dot(normed, w_key, preferred_element_type=jnp.float32)  32.3 us
    another operation x22, local copies, waits for them, and re-layouts  30.8 us
  transfers between devices with their start and end apart: 28, of which 24 were waited for; matrix products, arithmetic and copies ran while one was open for 23% of the time, Pallas kernels for 0%

profile of v1, /device:TPU:0, one launch (start us, length us, event | category | flops | bytes accessed | tf_op | source)
XLA Modules:
  0.0 759.4 jit_solution(10322608445339710844)
XLA Ops:
  54.9 26.2 %all-gather.6.cloned.1.call-done = bf16[1,8192,128]{2,1,0:T(8,128)(2,1)} async-done(((bf16[1,1024,128]{2,1,0:T(8,128)(2,1)}), bf16[1,8192,128]{2,1,0:T(8,128)(2,1)}) %all-gather.6.cloned.1.call-update) | async-done | bytes 2097168 | tf_op jit(solution)/shard_map/all_gather | solution.py:59
  81.1 30.2 %all-gather.8.cloned.1.call-done = bf16[1,8192,128]{2,1,0:T(8,128)(2,1)} async-done(((bf16[1,1024,128]{2,1,0:T(8,128)(2,1)}), bf16[1,8192,128]{2,1,0:T(8,128)(2,1)}) %all-gather.8.cloned.1.call-update) | async-done | bytes 2097168 | tf_op jit(solution)/shard_map/all_gather | solution.py:60
  112.9 170.8 %while.42 = (s32[]{:T(128)}, bf16[32,8192]{1,0:T(8,128)(2,1)S(1)}, bf16[4,32,8192]{2,1,0:T(8,128)(2,1)}, s32[]{:T(128)}, pred[]{:T(512)}, /*index=5*/bf16[4,32,8...) while((s32[]{:T(128)}, bf16[32,8192]{1,0:T(8,128)(2,1)S(1)}, ...), condition=%wide.region_6.7_spmd, body=%wide.region_0.6_spmd.sunk | while | flops 273452000 | bytes 19447128 | solution.py:91
  125.9 12.1 %collective-permute-done = bf16[32,8192]{1,0:T(8,128)(2,1)S(1)} collective-permute-done((bf16[32,8192]{1,0:T(8,128)(2,1)}, bf16[32,8192]{1,0:T(8,128)(2,1)S(1)}, u32[]{:S(2)}, u32[]{:S(2)}) %collective-permute-start) | collective-permute-done | bytes 524320 | tf_op jit(solution)/shard_map/while/body/eval_jaxpr/ppermute | solution.py:31
  154.0 11.3 %collective-permute-done = bf16[32,8192]{1,0:T(8,128)(2,1)S(1)} collective-permute-done((bf16[32,8192]{1,0:T(8,128)(2,1)}, bf16[32,8192]{1,0:T(8,128)(2,1)S(1)}, u32[]{:S(2)}, u32[]{:S(2)}) %collective-permute-start) | collective-permute-done | bytes 524320 | tf_op jit(solution)/shard_map/while/body/eval_jaxpr/ppermute | solution.py:31
  181.4 10.4 %collective-permute-done = bf16[32,8192]{1,0:T(8,128)(2,1)S(1)} collective-permute-done((bf16[32,8192]{1,0:T(8,128)(2,1)}, bf16[32,8192]{1,0:T(8,128)(2,1)S(1)}, u32[]{:S(2)}, u32[]{:S(2)}) %collective-permute-start) | collective-permute-done | bytes 524320 | tf_op jit(solution)/shard_map/while/body/eval_jaxpr/ppermute | solution.py:31
  221.3 12.4 %collective-permute-start = (bf16[32,8192]{1,0:T(8,128)(2,1)}, bf16[32,8192]{1,0:T(8,128)(2,1)S(1)}, u32[]{:S(2)}, u32[]{:S(2)}) collective-permute-start(bf16[32,8192]{1,0:T(8,128)(2,1)} %copy-done.8), channel_id=1, source_target_pairs={{0,8},{8,16},{16,24},{1,9},{9,17},{17,25},{2,10},{10,18},{18,26},{... | collective-permute-start | bytes 1572872 | tf_op jit(solution)/shard_map/while/body/eval_jaxpr/ppermute | solution.py:31
  263.7 12.9 %collective-permute-start = (bf16[32,8192]{1,0:T(8,128)(2,1)}, bf16[32,8192]{1,0:T(8,128)(2,1)S(1)}, u32[]{:S(2)}, u32[]{:S(2)}) collective-permute-start(bf16[32,8192]{1,0:T(8,128)(2,1)} %copy-done.8), channel_id=1, source_target_pairs={{0,8},{8,16},{16,24},{1,9},{9,17},{17,25},{2,10},{10,18},{18,26},{... | collective-permute-start | bytes 1572872 | tf_op jit(solution)/shard_map/while/body/eval_jaxpr/ppermute | solution.py:31
  286.1 315.4 %while.43 = (s32[]{:T(128)}, bf16[32,8192]{1,0:T(8,128)(2,1)}, f32[8192,128]{1,0:T(8,128)}, f32[8192,128]{1,0:T(8,128)}, f32[8192,128]{1,0:T(8,128)}, /*index=5*...) while((s32[]{:T(128)}, bf16[32,8192]{1,0:T(8,128)(2,1)}, ...), condition=%wide.region_17.18_spmd.clone, body=%wide.region_7.17_spmd.clone.sunk | while | flops 767129792 | bytes 145457920 | solution.py:126
  325.5 9.9 %select_add_fusion.7 = (f32[8192,128]{1,0:T(8,128)}, f32[8192,128]{1,0:T(8,128)}) fusion(f32[8192,128]{1,0:T(8,128)} %get-tuple-element.1022, f32[8192,128]{1,0:T(8,128)} %get-tuple-element.1106, pred[]{:T(512)S(6)} %compare.10, f32[8192,128]{1,0:T(8,128)} %get-tuple-element.1023, f32[8192,128]{1,0:T(8,128)} %get-tuple-element.1105), kind=kLoop, calls=%fused_computation.93.clone.1 | loop fusion | flops 4194304 | bytes 25165824 | tf_op jit(solution)/shard_map/while/body/eval_jaxpr/add | solution.py:117
  358.3 9.9 %select_add_fusion.7 = (f32[8192,128]{1,0:T(8,128)}, f32[8192,128]{1,0:T(8,128)}) fusion(f32[8192,128]{1,0:T(8,128)} %get-tuple-element.1022, f32[8192,128]{1,0:T(8,128)} %get-tuple-element.1106, pred[]{:T(512)S(6)} %compare.10, f32[8192,128]{1,0:T(8,128)} %get-tuple-element.1023, f32[8192,128]{1,0:T(8,128)} %get-tuple-element.1105), kind=kLoop, calls=%fused_computation.93.clone.1 | loop fusion | flops 4194304 | bytes 25165824 | tf_op jit(solution)/shard_map/while/body/eval_jaxpr/add | solution.py:117
  379.0 23.6 %collective-permute-done.1 = bf16[32,8192]{1,0:T(8,128)(2,1)S(1)} collective-permute-done((bf16[32,8192]{1,0:T(8,128)(2,1)S(1)}, bf16[32,8192]{1,0:T(8,128)(2,1)S(1)}, u32[]{:S(2)}, u32[]{:S(2)}) %collective-permute-start.1) | collective-permute-done | bytes 524320 | tf_op jit(solution)/shard_map/while/body/eval_jaxpr/ppermute | solution.py:31
  403.4 25.1 %conditional.6 = (bf16[32,8192]{1,0:T(8,128)(2,1)S(1)}, f32[8192,128]{1,0:T(8,128)}, f32[8192,128]{1,0:T(8,128)}, f32[8192,128]{1,0:T(8,128)}, f32[8192,128]{1,0:T(8,128)}) conditional(s32[]{:T(128)} %convert_element_type.326, () %tuple.115, (pred[]{:T(512)}, bf16[4,32,8192]{2,1,0:T(8,128)(2,1)}, s32[]{:T(128)}, bf16[32,8192]{1,0:T(8,128)(2,1)}, ...), branch_computations={%region_8.8_spmd, %region_9.16_spmd} | conditional | flops 758479040 | bytes 88309608 | solution.py:116
  430.9 9.9 %select_add_fusion.7 = (f32[8192,128]{1,0:T(8,128)}, f32[8192,128]{1,0:T(8,128)}) fusion(f32[8192,128]{1,0:T(8,128)} %get-tuple-element.1022, f32[8192,128]{1,0:T(8,128)} %get-tuple-element.1106, pred[]{:T(512)S(6)} %compare.10, f32[8192,128]{1,0:T(8,128)} %get-tuple-element.1023, f32[8192,128]{1,0:T(8,128)} %get-tuple-element.1105), kind=kLoop, calls=%fused_computation.93.clone.1 | loop fusion | flops 4194304 | bytes 25165824 | tf_op jit(solution)/shard_map/while/body/eval_jaxpr/add | solution.py:117
  453.1 25.1 %conditional.6 = (bf16[32,8192]{1,0:T(8,128)(2,1)S(1)}, f32[8192,128]{1,0:T(8,128)}, f32[8192,128]{1,0:T(8,128)}, f32[8192,128]{1,0:T(8,128)}, f32[8192,128]{1,0:T(8,128)}) conditional(s32[]{:T(128)} %convert_element_type.326, () %tuple.115, (pred[]{:T(512)}, bf16[4,32,8192]{2,1,0:T(8,128)(2,1)}, s32[]{:T(128)}, bf16[32,8192]{1,0:T(8,128)(2,1)}, ...), branch_computations={%region_8.8_spmd, %region_9.16_spmd} | conditional | flops 758479040 | bytes 88309608 | solution.py:116
  480.6 9.9 %select_add_fusion.7 = (f32[8192,128]{1,0:T(8,128)}, f32[8192,128]{1,0:T(8,128)}) fusion(f32[8192,128]{1,0:T(8,128)} %get-tuple-element.1022, f32[8192,128]{1,0:T(8,128)} %get-tuple-element.1106, pred[]{:T(512)S(6)} %compare.10, f32[8192,128]{1,0:T(8,128)} %get-tuple-element.1023, f32[8192,128]{1,0:T(8,128)} %get-tuple-element.1105), kind=kLoop, calls=%fused_computation.93.clone.1 | loop fusion | flops 4194304 | bytes 25165824 | tf_op jit(solution)/shard_map/while/body/eval_jaxpr/add | solution.py:117
  502.8 25.1 %conditional.6 = (bf16[32,8192]{1,0:T(8,128)(2,1)S(1)}, f32[8192,128]{1,0:T(8,128)}, f32[8192,128]{1,0:T(8,128)}, f32[8192,128]{1,0:T(8,128)}, f32[8192,128]{1,0:T(8,128)}) conditional(s32[]{:T(128)} %convert_element_type.326, () %tuple.115, (pred[]{:T(512)}, bf16[4,32,8192]{2,1,0:T(8,128)(2,1)}, s32[]{:T(128)}, bf16[32,8192]{1,0:T(8,128)(2,1)}, ...), branch_computations={%region_8.8_spmd, %region_9.16_spmd} | conditional | flops 758479040 | bytes 88309608 | solution.py:116
  530.3 9.9 %select_add_fusion.7 = (f32[8192,128]{1,0:T(8,128)}, f32[8192,128]{1,0:T(8,128)}) fusion(f32[8192,128]{1,0:T(8,128)} %get-tuple-element.1022, f32[8192,128]{1,0:T(8,128)} %get-tuple-element.1106, pred[]{:T(512)S(6)} %compare.10, f32[8192,128]{1,0:T(8,128)} %get-tuple-element.1023, f32[8192,128]{1,0:T(8,128)} %get-tuple-element.1105), kind=kLoop, calls=%fused_computation.93.clone.1 | loop fusion | flops 4194304 | bytes 25165824 | tf_op jit(solution)/shard_map/while/body/eval_jaxpr/add | solution.py:117
  552.4 25.1 %conditional.6 = (bf16[32,8192]{1,0:T(8,128)(2,1)S(1)}, f32[8192,128]{1,0:T(8,128)}, f32[8192,128]{1,0:T(8,128)}, f32[8192,128]{1,0:T(8,128)}, f32[8192,128]{1,0:T(8,128)}) conditional(s32[]{:T(128)} %convert_element_type.326, () %tuple.115, (pred[]{:T(512)}, bf16[4,32,8192]{2,1,0:T(8,128)(2,1)}, s32[]{:T(128)}, bf16[32,8192]{1,0:T(8,128)(2,1)}, ...), branch_computations={%region_8.8_spmd, %region_9.16_spmd} | conditional | flops 758479040 | bytes 88309608 | solution.py:116
  579.9 9.9 %select_add_fusion.7 = (f32[8192,128]{1,0:T(8,128)}, f32[8192,128]{1,0:T(8,128)}) fusion(f32[8192,128]{1,0:T(8,128)} %get-tuple-element.1022, f32[8192,128]{1,0:T(8,128)} %get-tuple-element.1106, pred[]{:T(512)S(6)} %compare.10, f32[8192,128]{1,0:T(8,128)} %get-tuple-element.1023, f32[8192,128]{1,0:T(8,128)} %get-tuple-element.1105), kind=kLoop, calls=%fused_computation.93.clone.1 | loop fusion | flops 4194304 | bytes 25165824 | tf_op jit(solution)/shard_map/while/body/eval_jaxpr/add | solution.py:117
  616.6 24.6 %reduce-scatter.5.cloned.1.call-done = bf16[1,1024,128]{2,1,0:T(8,128)(2,1)} async-done(((bf16[1,8192,128]{2,1,0:T(8,128)(2,1)}), bf16[1,1024,128]{2,1,0:T(8,128)(2,1)}) %reduce-scatter.5.cloned.1.call-update) | async-done | bytes 262160 | tf_op jit(solution)/shard_map/reduce_scatter | solution.py:130
  643.0 34.7 %reduce-scatter.7.cloned.1.call-done = bf16[1,1024,128]{2,1,0:T(8,128)(2,1)} async-done(((bf16[1,8192,128]{2,1,0:T(8,128)(2,1)}), bf16[1,1024,128]{2,1,0:T(8,128)(2,1)}) %reduce-scatter.7.cloned.1.call-update) | async-done | bytes 262160 | tf_op jit(solution)/shard_map/reduce_scatter | solution.py:133
  679.5 34.6 %reduce-scatter.9.cloned.1.call-done = bf16[1,1024,128]{2,1,0:T(8,128)(2,1)} async-done(((bf16[1,8192,128]{2,1,0:T(8,128)(2,1)}), bf16[1,1024,128]{2,1,0:T(8,128)(2,1)}) %reduce-scatter.9.cloned.1.call-update) | async-done | bytes 262160 | tf_op jit(solution)/shard_map/reduce_scatter | solution.py:136
  715.9 35.0 %reduce-scatter.11.cloned.1.call-done = bf16[1,1024,128]{2,1,0:T(8,128)(2,1)} async-done(((bf16[1,8192,128]{2,1,0:T(8,128)(2,1)}), bf16[1,1024,128]{2,1,0:T(8,128)(2,1)}) %reduce-scatter.11.cloned.1.call-update) | async-done | bytes 262160 | tf_op jit(solution)/shard_map/reduce_scatter | solution.py:139
  (362 shorter events, 474.6 us)
Async XLA Ops:
  7.2 47.7 %all-gather.4.cloned.1.call-start = ((), (), s32[]{:S(2)}) async-start(), calls=%async_computation.4 | async-start | bytes 2359296 | tf_op jit(solution)/shard_map/all_gather | solution.py:58
  7.9 73.1 %all-gather.6.cloned.1.call-start = ((), (), s32[]{:S(2)}) async-start(), calls=%async_computation.5 | async-start | bytes 2359296 | tf_op jit(solution)/shard_map/all_gather | solution.py:59
  8.7 102.6 %all-gather.8.cloned.1.call-start = ((), (), s32[]{:S(2)}) async-start(), calls=%async_computation.6 | async-start | bytes 2359296 | tf_op jit(solution)/shard_map/all_gather | solution.py:60
  9.4 631.8 %reduce-scatter.5.cloned.1.call-start = ((), (), s32[]{:S(2)}) async-start(), calls=%async_computation.7 | async-start | bytes 2359296 | tf_op jit(solution)/shard_map/reduce_scatter | solution.py:130
  19.0 15.0 %collective-permute-start.5 = (bf16[1,1024,128]{2,1,0:T(8,128)(2,1)S(1)}, bf16[1,1024,128]{2,1,0:T(8,128)(2,1)S(1)}, u32[]{:S(2)}, u32[]{:S(2)}) collective-permute-start(bf16[1,1024,128]{2,1,0:T(8,128)(2,1)S(1)} %collective-permute-done.3), channel_id=1, source_target_pairs={{0,7},{1,0},{2,1},{3,2},{4,3},{5,4},{6,5},{7,6},{8,15},{9,8},{10,9... | collective-permute-start | bytes 786440 | tf_op jit(solution)/shard_map/ppermute | solution.py:21
  30.2 13.5 %collective-permute-start.6 = (bf16[1,1024,128]{2,1,0:T(8,128)(2,1)S(1)}, bf16[1,1024,128]{2,1,0:T(8,128)(2,1)S(1)}, u32[]{:S(2)}, u32[]{:S(2)}) collective-permute-start(bf16[1,1024,128]{2,1,0:T(8,128)(2,1)S(1)} %collective-permute-done.4), channel_id=1, source_target_pairs={{0,1},{1,2},{2,3},{3,4},{4,5},{5,6},{6,7},{7,0},{8,9},{9,10},{10,1... | collective-permute-start | bytes 786440 | tf_op jit(solution)/shard_map/ppermute | solution.py:16
  34.0 14.2 %collective-permute-start.7 = (bf16[1,1024,128]{2,1,0:T(8,128)(2,1)S(1)}, bf16[1,1024,128]{2,1,0:T(8,128)(2,1)S(1)}, u32[]{:S(2)}, u32[]{:S(2)}) collective-permute-start(bf16[1,1024,128]{2,1,0:T(8,128)(2,1)S(1)} %collective-permute-done.5), channel_id=1, source_target_pairs={{0,7},{1,0},{2,1},{3,2},{4,3},{5,4},{6,5},{7,6},{8,15},{9,8},{10,9... | collective-permute-start | bytes 786440 | tf_op jit(solution)/shard_map/ppermute | solution.py:21
  124.6 13.4 %collective-permute-start = (bf16[32,8192]{1,0:T(8,128)(2,1)}, bf16[32,8192]{1,0:T(8,128)(2,1)S(1)}, u32[]{:S(2)}, u32[]{:S(2)}) collective-permute-start(bf16[32,8192]{1,0:T(8,128)(2,1)} %copy-done.8), channel_id=1, source_target_pairs={{0,8},{8,16},{16,24},{1,9},{9,17},{17,25},{2,10},{10,18},{18,26},{... | collective-permute-start | bytes 1572872 | tf_op jit(solution)/shard_map/while/body/eval_jaxpr/ppermute | solution.py:31
  149.7 15.6 %collective-permute-start = (bf16[32,8192]{1,0:T(8,128)(2,1)}, bf16[32,8192]{1,0:T(8,128)(2,1)S(1)}, u32[]{:S(2)}, u32[]{:S(2)}) collective-permute-start(bf16[32,8192]{1,0:T(8,128)(2,1)} %copy-done.8), channel_id=1, source_target_pairs={{0,8},{8,16},{16,24},{1,9},{9,17},{17,25},{2,10},{10,18},{18,26},{... | collective-permute-start | bytes 1572872 | tf_op jit(solution)/shard_map/while/body/eval_jaxpr/ppermute | solution.py:31
  177.0 14.8 %collective-permute-start = (bf16[32,8192]{1,0:T(8,128)(2,1)}, bf16[32,8192]{1,0:T(8,128)(2,1)S(1)}, u32[]{:S(2)}, u32[]{:S(2)}) collective-permute-start(bf16[32,8192]{1,0:T(8,128)(2,1)} %copy-done.8), channel_id=1, source_target_pairs={{0,8},{8,16},{16,24},{1,9},{9,17},{17,25},{2,10},{10,18},{18,26},{... | collective-permute-start | bytes 1572872 | tf_op jit(solution)/shard_map/while/body/eval_jaxpr/ppermute | solution.py:31
  203.5 13.8 %collective-permute-start = (bf16[32,8192]{1,0:T(8,128)(2,1)}, bf16[32,8192]{1,0:T(8,128)(2,1)S(1)}, u32[]{:S(2)}, u32[]{:S(2)}) collective-permute-start(bf16[32,8192]{1,0:T(8,128)(2,1)} %copy-done.8), channel_id=1, source_target_pairs={{0,8},{8,16},{16,24},{1,9},{9,17},{17,25},{2,10},{10,18},{18,26},{... | collective-permute-start | bytes 1572872 | tf_op jit(solution)/shard_map/while/body/eval_jaxpr/ppermute | solution.py:31
  221.3 21.3 %collective-permute-start = (bf16[32,8192]{1,0:T(8,128)(2,1)}, bf16[32,8192]{1,0:T(8,128)(2,1)S(1)}, u32[]{:S(2)}, u32[]{:S(2)}) collective-permute-start(bf16[32,8192]{1,0:T(8,128)(2,1)} %copy-done.8), channel_id=1, source_target_pairs={{0,8},{8,16},{16,24},{1,9},{9,17},{17,25},{2,10},{10,18},{18,26},{... | collective-permute-start | bytes 1572872 | tf_op jit(solution)/shard_map/while/body/eval_jaxpr/ppermute | solution.py:31
  246.6 13.2 %collective-permute-start = (bf16[32,8192]{1,0:T(8,128)(2,1)}, bf16[32,8192]{1,0:T(8,128)(2,1)S(1)}, u32[]{:S(2)}, u32[]{:S(2)}) collective-permute-start(bf16[32,8192]{1,0:T(8,128)(2,1)} %copy-done.8), channel_id=1, source_target_pairs={{0,8},{8,16},{16,24},{1,9},{9,17},{17,25},{2,10},{10,18},{18,26},{... | collective-permute-start | bytes 1572872 | tf_op jit(solution)/shard_map/while/body/eval_jaxpr/ppermute | solution.py:31
  263.7 20.0 %collective-permute-start = (bf16[32,8192]{1,0:T(8,128)(2,1)}, bf16[32,8192]{1,0:T(8,128)(2,1)S(1)}, u32[]{:S(2)}, u32[]{:S(2)}) collective-permute-start(bf16[32,8192]{1,0:T(8,128)(2,1)} %copy-done.8), channel_id=1, source_target_pairs={{0,8},{8,16},{16,24},{1,9},{9,17},{17,25},{2,10},{10,18},{18,26},{... | collective-permute-start | bytes 1572872 | tf_op jit(solution)/shard_map/while/body/eval_jaxpr/ppermute | solution.py:31
  295.0 18.3 %collective-permute-start.1 = (bf16[32,8192]{1,0:T(8,128)(2,1)S(1)}, bf16[32,8192]{1,0:T(8,128)(2,1)S(1)}, u32[]{:S(2)}, u32[]{:S(2)}) collective-permute-start(bf16[32,8192]{1,0:T(8,128)(2,1)S(1)} %get-tuple-element.1017), channel_id=1, source_target_pairs={{8,0},{16,8},{24,16},{9,1},{17,9},{25,17},{10,2},{18,10},{26,18},{... | collective-permute-start | bytes 1572872 | tf_op jit(solution)/shard_map/while/body/eval_jaxpr/ppermute | solution.py:31
  323.1 23.1 %collective-permute-start.1 = (bf16[32,8192]{1,0:T(8,128)(2,1)S(1)}, bf16[32,8192]{1,0:T(8,128)(2,1)S(1)}, u32[]{:S(2)}, u32[]{:S(2)}) collective-permute-start(bf16[32,8192]{1,0:T(8,128)(2,1)S(1)} %get-tuple-element.1017), channel_id=1, source_target_pairs={{8,0},{16,8},{24,16},{9,1},{17,9},{25,17},{10,2},{18,10},{26,18},{... | collective-permute-start | bytes 1572872 | tf_op jit(solution)/shard_map/while/body/eval_jaxpr/ppermute | solution.py:31
  355.9 46.7 %collective-permute-start.1 = (bf16[32,8192]{1,0:T(8,128)(2,1)S(1)}, bf16[32,8192]{1,0:T(8,128)(2,1)S(1)}, u32[]{:S(2)}, u32[]{:S(2)}) collective-permute-start(bf16[32,8192]{1,0:T(8,128)(2,1)S(1)} %get-tuple-element.1017), channel_id=1, source_target_pairs={{8,0},{16,8},{24,16},{9,1},{17,9},{25,17},{10,2},{18,10},{26,18},{... | collective-permute-start | bytes 1572872 | tf_op jit(solution)/shard_map/while/body/eval_jaxpr/ppermute | solution.py:31
  428.6 23.7 %collective-permute-start.1 = (bf16[32,8192]{1,0:T(8,128)(2,1)S(1)}, bf16[32,8192]{1,0:T(8,128)(2,1)S(1)}, u32[]{:S(2)}, u32[]{:S(2)}) collective-permute-start(bf16[32,8192]{1,0:T(8,128)(2,1)S(1)} %get-tuple-element.1017), channel_id=1, source_target_pairs={{8,0},{16,8},{24,16},{9,1},{17,9},{25,17},{10,2},{18,10},{26,18},{... | collective-permute-start | bytes 1572872 | tf_op jit(solution)/shard_map/while/body/eval_jaxpr/ppermute | solution.py:31
  478.2 23.7 %collective-permute-start.1 = (bf16[32,8192]{1,0:T(8,128)(2,1)S(1)}, bf16[32,8192]{1,0:T(8,128)(2,1)S(1)}, u32[]{:S(2)}, u32[]{:S(2)}) collective-permute-start(bf16[32,8192]{1,0:T(8,128)(2,1)S(1)} %get-tuple-element.1017), channel_id=1, source_target_pairs={{8,0},{16,8},{24,16},{9,1},{17,9},{25,17},{10,2},{18,10},{26,18},{... | collective-permute-start | bytes 1572872 | tf_op jit(solution)/shard_map/while/body/eval_jaxpr/ppermute | solution.py:31
  527.9 23.7 %collective-permute-start.1 = (bf16[32,8192]{1,0:T(8,128)(2,1)S(1)}, bf16[32,8192]{1,0:T(8,128)(2,1)S(1)}, u32[]{:S(2)}, u32[]{:S(2)}) collective-permute-start(bf16[32,8192]{1,0:T(8,128)(2,1)S(1)} %get-tuple-element.1017), channel_id=1, source_target_pairs={{8,0},{16,8},{24,16},{9,1},{17,9},{25,17},{10,2},{18,10},{26,18},{... | collective-permute-start | bytes 1572872 | tf_op jit(solution)/shard_map/while/body/eval_jaxpr/ppermute | solution.py:31
  577.6 23.1 %collective-permute-start.1 = (bf16[32,8192]{1,0:T(8,128)(2,1)S(1)}, bf16[32,8192]{1,0:T(8,128)(2,1)S(1)}, u32[]{:S(2)}, u32[]{:S(2)}) collective-permute-start(bf16[32,8192]{1,0:T(8,128)(2,1)S(1)} %get-tuple-element.1017), channel_id=1, source_target_pairs={{8,0},{16,8},{24,16},{9,1},{17,9},{25,17},{10,2},{18,10},{26,18},{... | collective-permute-start | bytes 1572872 | tf_op jit(solution)/shard_map/while/body/eval_jaxpr/ppermute | solution.py:31
  605.2 72.5 %reduce-scatter.7.cloned.1.call-start = ((), (), s32[]{:S(2)}) async-start(), calls=%async_computation.8 | async-start | bytes 2359296 | tf_op jit(solution)/shard_map/reduce_scatter | solution.py:133
  609.0 105.1 %reduce-scatter.9.cloned.1.call-start = ((), (), s32[]{:S(2)}) async-start(), calls=%async_computation.9 | async-start | bytes 2359296 | tf_op jit(solution)/shard_map/reduce_scatter | solution.py:136
  612.8 138.0 %reduce-scatter.11.cloned.1.call-start = ((), (), s32[]{:S(2)}) async-start(), calls=%async_computation.10 | async-start | bytes 2359296 | tf_op jit(solution)/shard_map/reduce_scatter | solution.py:139
  (45 other events, 255.8 us)
Sparse Core Ops, SparseCore 0:
  9.6 40.9 all-gather.3
  52.2 28.7 all-gather.5
  82.7 28.5 all-gather.7
  605.3 35.8 reduce-scatter.4
  643.3 34.3 reduce-scatter.6
  679.8 34.2 reduce-scatter.8
  716.4 34.3 reduce-scatter.10
